TPU v7x, 32 devices: a whole 2x2x4 slice. The times are simulated.
32 devices in a mesh: rays: 8 (over z, x), views: 4 (over y, core).
Axes of the slice: x: 2, y: 2, z: 4, core: 2. Of those that a mesh axis runs over, the one named last changes fastest.
Arguments:
- master: float32 [11384], P('rays')
- first_moment: float32 [11384], P('rays'), may hold values from -0.75 to 0.75
- second_moment: float32 [11384], P('rays'), may hold values from 0.001 to 0.01
- step_count: int32 [1], replicated, may hold values from 2 to 20
- feature_maps: bfloat16 [12, 35, 12032], P('views'), may hold values from -6 to 6
- pixel_index: int32 [24576, 12], P('rays', 'views'), may hold values from 0 to 12031
- visible: int32 [24576, 12], P('rays', 'views'), may hold values from 0 to 1, as said below
- deltas: float32 [128, 192], P('rays'), may hold values from 0.002 to 0.02
- targets: float32 [128, 3], P('rays'), may hold values from -3 to 3
- scene_id: int32 [128], P('rays'), may hold values from 0 to 7
- scene_weight: int32 [8], replicated, may hold values from 1 to 4
Outputs:
- loss: float32 [], replicated
- master_new: float32 [11384], P('rays')
- first_new: float32 [11384], P('rays')
- second_new: float32 [11384], P('rays')
Inputs may be any that keep to these rules, and one draw needn't show every extreme that they name: Every sample is visible in at least one of the first 10 view slots; the last two slots are never visible.
All inputs are finite; a program needn't handle non-finite values.
Results may differ from a plain program's by a relative error of at most 0.00077.
Values may be sent and summed in bfloat16 or wider, within the bound.
No kernel may reach another device: no remote copies, remote signals or barrier semaphores. Data moves between devices by JAX's collectives and lax.ppermute only.
A program may use at most 128 MiB of HBM per device.

v0:
```python
import jax
import jax.numpy as jnp
from jax import lax
from jax.experimental import pallas as pl
from jax.experimental.pallas import tpu as pltpu
from jax.sharding import PartitionSpec as P


F32 = jnp.float32
BF16 = jnp.bfloat16
SEEN_VIEWS = 10
CHANNELS = 35
STRIP = 40
BAND = 32
SEEN_SHIFT = 14
SEEN_BIT = 1 << SEEN_SHIFT
GATHER_TILE = 768
RAY = 192
CHUNK = 2 * RAY
PASSES = 1
TILE = 128
MOMENT_DECAY = 0.5
SQUARE_DECAY = 0.5
LEARNING_RATE = 0.05
WEIGHT_DECAY = 0.01
EPSILON = 1e-08
NN = (((1,), (0,)), ((), ()))
NT = (((1,), (1,)), ((), ()))
TN = (((0,), (0,)), ((), ()))


def dot(left, right, dims=NN):
    return lax.dot_general(left, right, dims, preferred_element_type=F32)


def parts(value, count):
    out = []
    for step in range(count):
        piece = value.astype(BF16)
        out.append(piece)
        if step + 1 < count:
            value = value - piece.astype(F32)
    return out


def dot_left(value, right, dims, count=PASSES):
    return sum(dot(piece, right, dims) for piece in parts(value, count))


def dot_right(left, value, dims, count=PASSES):
    return sum(dot(left, piece, dims) for piece in parts(value, count))


def elu_pair(value):
    slope = jnp.exp(jnp.minimum(value, 0.0))
    return jnp.maximum(value, 0.0) + (slope - 1.0), slope


def iota(shape, axis):
    return lax.broadcasted_iota(jnp.int32, shape, axis)


def table_rows(blocks):
    return BAND * blocks + 16 * (-(-blocks // 4))


def stack_maps(map_ref, stacked, view):
    channels, pixels = map_ref.shape[1:]
    blocks = pixels // 256
    blank = jnp.zeros((4, 256), F32)
    for block in range(blocks):
        lanes = slice(256 * block, 256 * (block + 1))
        stacked[view, BAND * block : BAND * (block + 1), :] = map_ref[view, 0:BAND, lanes]
    for first in range(0, blocks, 4):
        strips = []
        for block in range(first, first + 4):
            if block < blocks:
                lanes = slice(256 * block, 256 * (block + 1))
                strips.append(map_ref[view, BAND:channels, lanes].astype(F32))
                strips.append(blank[: BAND + 4 - channels])
            else:
                strips.append(blank)
        at = BAND * blocks + 4 * first
        stacked[view, at : at + 16, :] = jnp.concatenate(strips, axis=0).astype(BF16)


def gather_kernel(views, tile, count, *refs):
    packed_refs, source = refs[1 : 1 + count], refs[1 + count]
    outs, stacked = refs[2 + count : -1], refs[-1]
    blocks = source.shape[2] // 256

    @pl.when(pl.program_id(0) == 0)
    def _():
        for view in range(views):
            stack_maps(source, stacked, view)

    row = iota((8, tile), 0)
    upper = jnp.where(row < 4, 0, 1)
    for packed_ref, out_ref in zip(packed_refs, outs):
        strips = []
        for view in range(views):
            packed = packed_ref[view : view + 1, :]
            index = packed & (SEEN_BIT - 1)
            high = jnp.broadcast_to(index >> 8, (8, tile))
            low = jnp.broadcast_to(index & 255, (256, tile))
            picked = (iota((256, tile), 0) == low).astype(F32).astype(BF16)
            found = dot(stacked[view], picked)
            totals = [jnp.zeros((8, tile), F32)] * (BAND // 8)
            for block in range(blocks):
                here = high == block
                for part in range(BAND // 8):
                    at = BAND * block + 8 * part
                    totals[part] = jnp.where(here, found[at : at + 8], totals[part])
            last = jnp.zeros((8, tile), F32)
            half = high - upper
            for pair in range(-(-blocks // 2)):
                at = BAND * blocks + 8 * pair
                last = jnp.where(half == 2 * pair, found[at : at + 8], last)
            last = last + pltpu.roll(last, 4, 0)
            seen = jnp.broadcast_to((packed >> SEEN_SHIFT).astype(F32), (8, tile))
            last = jnp.where(row == CHANNELS - BAND, 1.0, last)
            last = jnp.where(row == CHANNELS - BAND + 1, seen, last)
            strips += totals + [jnp.where(row > CHANNELS - BAND + 1, 0.0, last)]
        out_ref[0] = jnp.concatenate(strips, axis=0).astype(BF16)


def gather_rows(packed, source, me, group, ways):
    views, points = packed.shape
    tile = GATHER_TILE
    own = points // group
    tiles = own // tile
    count = len(ways)
    part = lambda k: pl.BlockSpec((views, tile), lambda t, me: (0, (me[0] ^ k) * tiles + t))
    whole = lambda shape: pl.BlockSpec(shape, lambda t, me: (0, 0, 0))
    outs = [jax.ShapeDtypeStruct((1, views * STRIP, own), BF16)] * count
    out_specs = [pl.BlockSpec((1, views * STRIP, tile), lambda t, me: (0, 0, t))] * count
    table = (views, table_rows(source.shape[2] // 256), 256)
    flops = 2 * views * own * count * table[1] * 256
    return pl.pallas_call(
        lambda *refs: gather_kernel(views, tile, count, *refs),
        out_shape=outs,
        grid_spec=pltpu.PrefetchScalarGridSpec(
            num_scalar_prefetch=1,
            grid=(tiles,),
            in_specs=[part(k) for k in ways] + [whole(source.shape)],
            out_specs=out_specs,
            scratch_shapes=[pltpu.VMEM(table, BF16)],
        ),
        compiler_params=pltpu.CompilerParams(vmem_limit_bytes=32 * 1024 * 1024),
        cost_estimate=pl.CostEstimate(
            flops=flops, bytes_accessed=source.size * 2, transcendentals=0
        ),
    )(me, *([packed] * count), source)


def roll(value, shift):
    return pltpu.roll(value, shift % 128, 1)


def unpack(a_ref, r64, r32, r16):
    for b in range(2):
        r64[pl.ds(b, 18, stride=2), :] = roll(a_ref[0:18, :], -64 * b)
    for b in range(4):
        r32[pl.ds(b, 33, stride=4), :] = roll(a_ref[18:51, :], -32 * b)
    for b in range(8):
        r16[pl.ds(b, 39, stride=8), :] = roll(a_ref[50:89, :], -16 * b)


def assemble(place, shard, shard_refs, a_ref):
    a_ref[...] = jnp.zeros_like(a_ref)
    shards, rows, _ = shard_refs.shape
    for k in range(shards):
        start = (place ^ k) * shard
        shift = start & 127
        value = pltpu.roll(shard_refs[k].astype(F32), shift, 1)
        keep = iota((rows, 128), 1) >= shift
        first = start >> 7
        a_ref[pl.ds(first, rows), :] += jnp.where(keep, value, 0.0)
        a_ref[pl.ds(first + 1, rows), :] += jnp.where(keep, 0.0, value)


def repeat(weight, out_ref, times):
    out_ref[...] = jnp.zeros_like(out_ref)
    rows, width = weight.shape
    wide = widen(weight)
    for part in range(times):
        tile, shift = divmod(width * part, 128)
        out_ref[rows * part : rows * (part + 1), 128 * tile : 128 * (tile + 1)] = roll(
            wide, shift
        ).astype(BF16)


def blocks_sum(ref, rows, width, times):
    total = sum(
        roll(ref[rows * part : rows * (part + 1), :], -width * part) for part in range(times)
    )
    return jnp.where(iota((rows, 128), 1) < width, total, 0.0)


def column(rows):
    return rows.T[:, 0:1]


def main_kernel(views, shard, me_ref, *refs):
    shard_refs, refs = refs[0], refs[1:]
    (
    x0,
    x1,
    x2,
    x3,
    delta_ref,
    target_ref,
    weight_ref,
    out_ref,
    sums_ref,
    a_ref,
    r64,
    r32,
    r16,
    xs,
    hb,
    he,
    ff,
    fe,
    jb,
    ib,
    ie,
    ee,
    dl,
    di,
    df,
    dh,
    blk,
    w2t_s,
    w2_s,
    u1t_s,
    u1_s,
    u2t_s,
    u2_s,
    tri_s,
    g64,
    g32,
    g16,
    gw1,
    gw2,
    gu1,
    gu2,
    gb2,
    gc1,
    gc2,
    gd1,
    gs2,
    gdd,
    loss_s,
    ) = refs
    step = pl.program_id(0)
    n = CHUNK
    lane = iota((1, n), 1)
    first_ray = lane < RAY
    me = me_ref[0]

    @pl.when(step == 0)
    def _():
        assemble(me_ref[1], shard, shard_refs, a_ref)
        unpack(a_ref, r64, r32, r16)
        for ref in (g64, g32, g16, gw1, gw2, gu1, gu2, gb2, gc1, gc2, gd1, gs2, gdd, loss_s):
            ref[...] = jnp.zeros_like(ref)
        before = (iota((n, n), 0) < iota((n, n), 1)) & (
            (iota((n, n), 0) < RAY) == (iota((n, n), 1) < RAY)
        )
        tri_s[...] = before.astype(F32).astype(BF16)
        w1t = jnp.where(iota((64, 128), 1) < 36, 1.0, 0.0) * jnp.concatenate(
            [r64[0:36, :], jnp.zeros((92, 128), F32)], axis=0
        ).T[:64]
        for view in range(views):
            blk[64 * view : 64 * (view + 1), :] = roll(w1t, STRIP * view).astype(BF16)
        w2 = r32[0:64, :][:, :32]
        u1a = r32[65:97, :][:, :32]
        u2 = r16[4:36, :][:, :16]
        repeat(w2.T, w2t_s, views)
        repeat(w2, w2_s, views)
        repeat(u1a.T, u1t_s, views)
        repeat(u1a, u1_s, views)
        repeat(u2.T, u2t_s, views)
        repeat(u2, u2_s, views)

    for k, ref in enumerate((x0, x1, x2, x3)):
        xs[me ^ k] = ref[0]

    b2 = column(r32[64:72, :])[:32]
    u1b = r32[97:129, :][:, :32]
    u1bt = u1b.T.astype(BF16)
    u1b = u1b.astype(BF16)
    c1 = column(r32[129:137, :])[:32]
    c2 = column(r16[36:44, :])[:16]
    keep16 = iota((48, 128), 1) < 16
    qkv = sum(
        roll(jnp.where(keep16, r16[pl.ds(37 + a, 48, stride=4), :], 0.0), 16 * a) for a in range(4)
    )
    wq, wk, wv = qkv[0:16], qkv[16:32], qkv[32:48]
    wqb = wq[:, :64].astype(BF16)
    wqt = wq[:, :64].T.astype(BF16)
    wk_of = [roll(wk, 64 * r).astype(BF16) for r in range(2)]
    wv_of = [roll(wv, 64 * r).astype(BF16) for r in range(2)]
    wo = r16[229:293, :][:, :16]
    wob = wo.astype(BF16)
    wot = wo.T.astype(BF16)
    s1 = r16[293:309, :][:, :16]
    s1b = s1.astype(BF16)
    s1t = s1.T.astype(BF16)
    d1 = column(r16[309:317, :])[:16]
    s2 = column(r16[310:318, :])[:16]
    d2 = r16[311:312, 0:1]

    def strip_of(group, local, lanes):
        at = STRIP * local + 32
        strip = xs[group, at : at + 8, lanes].astype(F32)
        return strip[0:3], strip[4:5]

    def stack(values):
        return jnp.concatenate(values, axis=0) if len(values) > 1 else values[0]

    def cut(value, rows, local):
        return value[rows * local : rows * (local + 1)]

    counts = [min(views, SEEN_VIEWS - at) for at in range(0, SEEN_VIEWS, views)]

    m = TILE
    lane_tiles = [slice(at, at + m) for at in range(0, n, m)]
    join = lambda values: jnp.concatenate(values, axis=1) if len(values) > 1 else values[0]

    def forward_tile(lanes):
        sum1 = jnp.zeros((32, m), F32)
        sum2 = jnp.zeros((32, m), F32)
        seen = jnp.zeros((1, m), F32)
        for group, count in enumerate(counts):
            wide, thin = 64 * count, 32 * count
            value, slope = elu_pair(dot(blk[0:wide, 0 : views * STRIP], xs[group, :, lanes]))
            hidden = value.astype(BF16)
            hb[group, 0:wide, lanes] = hidden
            he[group, 0:wide, lanes] = slope
            value, slope = elu_pair(dot(w2t_s[0:thin, 0:wide], hidden) + stack([b2] * count))
            ff[group, 0:thin, lanes] = value
            fe[group, 0:thin, lanes] = slope
            for local in range(count):
                vis = strip_of(group, local, lanes)[1]
                one = cut(value, 32, local)
                part = vis * one
                sum1 = sum1 + part
                sum2 = sum2 + part * one
                seen = seen + vis
        average = sum1 / seen
        variance = sum2 / seen - average * average
        variance_low = variance.astype(BF16)
        shared = dot(u1bt, variance_low) + c1
        num = jnp.zeros((16, m), F32)
        den = jnp.zeros((16, m), F32)
        col = jnp.zeros((3, m), F32)
        for group, count in enumerate(counts):
            thin, low = 32 * count, 16 * count
            feature = ff[group, 0:thin, lanes]
            joined = (feature - stack([average] * count)).astype(BF16)
            jb[group, 0:thin, lanes] = joined
            value, slope = elu_pair(dot(u1t_s[0:thin, 0:thin], joined) + stack([shared] * count))
            inner = value.astype(BF16)
            ib[group, 0:thin, lanes] = inner
            ie[group, 0:thin, lanes] = slope
            raw = jnp.exp(dot(u2t_s[0:low, 0:thin], inner) + stack([c2] * count))
            for local in range(count):
                rgb, vis = strip_of(group, local, lanes)
                e = vis * cut(raw, 16, local)
                ee[group, 16 * local : 16 * (local + 1), lanes] = e
                num = num + e * feature[32 * local : 32 * local + 16]
                den = den + e
                col = col + e[0:1] * rgb
        return average, 1.0 / seen, variance_low, num, den, col

    done = [forward_tile(lanes) for lanes in lane_tiles]
    average, inv_seen, variance_low, num, den, col = [join(list(x)) for x in zip(*done)]

    inv = 1.0 / den
    tokens = num / den
    colour = col / den[0:1]
    token_low = tokens.astype(BF16)
    token_t = tokens.T.astype(BF16)
    halves = [token_t[RAY * r : RAY * (r + 1)] for r in range(2)]
    query = dot(wqt, token_low).astype(BF16).astype(F32) * 0.25
    kk_f = dot(halves[0], wk_of[0]) + dot(halves[1], wk_of[1])
    vv_f = dot(halves[0], wv_of[0]) + dot(halves[1], wv_of[1])
    kk = kk_f.astype(BF16)
    vv = vv_f.astype(BF16)
    kkt = kk.astype(F32).T.astype(BF16)
    vvt = vv.astype(F32).T.astype(BF16)

    def spread(value, head):
        mine = value[16 * head : 16 * (head + 1)].astype(F32)
        one = jnp.where(first_ray, mine, 0.0)
        rows = []
        for part in (one, mine - one):
            rows += [jnp.zeros((16 * head, n), BF16)] if head else []
            rows.append(part.astype(BF16))
            rows += [jnp.zeros((48 - 16 * head, n), BF16)] if head < 3 else []
        return jnp.concatenate(rows, axis=0)

    def fold(value):
        return jnp.where(first_ray, value[:16], value[16:])

    def head_rows(value, head):
        at = 16 * head
        return jnp.concatenate([value[at : at + 16], value[64 + at : 80 + at]], axis=0)

    probs = []
    lows = []
    attended = []
    query_of = []
    for head in range(4):
        q_head = spread(query, head)
        query_of.append(q_head)
        tiles = []
        for at in range(0, n, 128):
            score = dot(kk, q_head[:, at : at + 128])
            score = jnp.exp(score - jnp.max(score, axis=0, keepdims=True))
            tiles.append(score * (1.0 / jnp.sum(score, axis=0, keepdims=True)))
        probs.append(tiles)
        low = jnp.concatenate([tile.astype(BF16) for tile in tiles], axis=1)
        lows.append(low)
        attended.append(fold(dot(head_rows(vvt, head), low)))
    raw_attended = attended
    attended = jnp.concatenate(attended, axis=0).astype(BF16)
    mixed = tokens + dot(wot, attended)
    mixed_low = mixed.astype(BF16)
    value, s_slope = elu_pair(dot(s1t, mixed_low) + d1)
    act = value.astype(BF16).astype(F32)
    z = jnp.sum(act * s2, axis=0, keepdims=True) + d2
    delta = delta_ref[0]
    ez = jnp.exp(-jnp.abs(z))
    density = jnp.maximum(z, 0.0) + jnp.log1p(ez)
    sigmoid = jnp.where(z >= 0.0, 1.0, ez) / (1.0 + ez)
    optical = density * delta
    tri = tri_s[...]

    def exact_rows(value):
        pad = jnp.zeros((13, n), F32)
        return jnp.concatenate([p.astype(F32) for p in parts(value, 3)] + [pad], axis=0).astype(BF16)

    before = jnp.sum(dot(exact_rows(optical), tri), axis=0, keepdims=True)
    through = jnp.exp(-before)
    gone = jnp.exp(-optical)
    render = through * (1.0 - gone)
    drawn = render * colour
    targets = target_ref[0]
    rweight = weight_ref[0]
    d_pixel = jnp.zeros((3, n), F32)
    loss = jnp.zeros((1, 1), F32)
    for r in range(2):
        mask = first_ray if r == 0 else jnp.logical_not(first_ray)
        pixel = jnp.sum(jnp.where(mask, drawn, 0.0), axis=1, keepdims=True)
        miss = pixel - targets[0:3, r : r + 1]
        scale = rweight[0:1, r : r + 1]
        loss = loss + scale * jnp.sum(miss * miss, axis=0, keepdims=True)
        d_pixel = d_pixel + jnp.where(mask, 2.0 * scale * miss, 0.0)
    place = iota((8, 128), 1) + 128 * iota((8, 128), 0)
    loss_s[...] += jnp.where(place == 0, loss, 0.0) + jnp.where(
        place == 1, rweight[0:1, 0:1] + rweight[0:1, 1:2], 0.0
    )

    d_render = jnp.sum(d_pixel * colour, axis=0, keepdims=True)
    d_colour = d_pixel * render
    d_before = -render * d_render
    d_optical = through * gone * d_render + jnp.sum(
        dot(exact_rows(d_before), tri, NT), axis=0, keepdims=True
    )
    dz = d_optical * delta * sigmoid
    gs2[...] += act * dz
    gdd[...] += jnp.where(iota((8, n), 0) == 0, dz, 0.0)
    d_pre = s2 * dz * s_slope
    gd1[...] += d_pre
    g16[293:309, :] += widen(dot_right(mixed_low, d_pre, NT))
    d_mixed = dot_right(s1b, d_pre, NN)
    g16[229:293, :] += widen(dot_right(attended, d_mixed, NT))
    d_att = dot_right(wob, d_mixed, NN)
    d_query = []
    d_kk = jnp.zeros((RAY, 128), F32)
    d_vv = jnp.zeros((RAY, 128), F32)
    for head in range(4):
        mine = d_att[16 * head : 16 * (head + 1)]
        shift = jnp.sum(mine * raw_attended[head], axis=0, keepdims=True)
        d_head = spread(d_att, head)
        d_vv = d_vv + dot(lows[head], d_head, NT)
        tiles = []
        for place, prob in enumerate(probs[head]):
            at = slice(128 * place, 128 * (place + 1))
            tiles.append((prob * (dot(vv, d_head[:, at]) - shift[:, at])).astype(BF16))
        d_score = jnp.concatenate(tiles, axis=1)
        d_query.append(fold(dot(head_rows(kkt, head), d_score)) * 0.25)
        d_kk = d_kk + dot(d_score, query_of[head], NT)
    d_query = jnp.concatenate(d_query, axis=0)
    gq = dot_right(token_low, d_query, NT)
    gk = [dot_right(halves[r], d_kk, TN) for r in range(2)]
    gv = [dot_right(halves[r], d_vv, TN) for r in range(2)]
    wide = jnp.concatenate([widen(gq), gk[0] + roll(gk[1], 64), gv[0] + roll(gv[1], 64)], axis=0)
    for a in range(4):
        at = pl.ds(37 + a, 48, stride=4)
        g16[at, :] += jnp.where(keep16, roll(wide, -16 * a), 0.0)
    d_halves = [
        dot_left(d_kk, wk_of[r], NT) + dot_left(d_vv, wv_of[r], NT) for r in range(2)
    ]
    d_tokens = d_mixed + dot_right(wqb, d_query, NN) + jnp.concatenate(d_halves, axis=0).T
    d_num = d_tokens * inv
    d_den = -d_num * tokens
    d_col = d_colour * inv[0:1]
    d_den0 = -jnp.sum(d_col * colour, axis=0, keepdims=True)
    row16 = iota((16, n), 0)
    d_den = d_den + jnp.where(row16 == 0, d_den0, 0.0)

    def backward_tile(lanes):
        own_num, own_den, own_col = d_num[:, lanes], d_den[:, lanes], d_col[:, lanes]
        d_average = jnp.zeros((32, m), F32)
        d_shared = jnp.zeros((32, m), F32)
        sum_c2 = jnp.zeros((16, m), F32)
        for group, count in enumerate(counts):
            thin, low = 32 * count, 16 * count
            d_logit = []
            for local in range(count):
                at = slice(16 * local, 16 * (local + 1))
                rgb, _ = strip_of(group, local, lanes)
                e = ee[group, at, lanes]
                d_e = own_num * ff[group, 32 * local : 32 * local + 16, lanes] + own_den
                shade = jnp.sum(own_col * rgb, axis=0, keepdims=True)
                d_e = d_e + jnp.where(row16[:, :m] == 0, shade, 0.0)
                d_logit.append(d_e * e)
                sum_c2 = sum_c2 + d_logit[-1]
                ee[group, at, lanes] = own_num * e
            piece = stack(d_logit).astype(BF16)
            dl[group, 0:low, lanes] = piece
            d_inner = dot(u2_s[0:thin, 0:low], piece) * ie[group, 0:thin, lanes]
            piece = d_inner.astype(BF16)
            di[group, 0:thin, lanes] = piece
            d_joined = dot(u1_s[0:thin, 0:thin], piece)
            ie[group, 0:thin, lanes] = d_joined
            for local in range(count):
                d_shared = d_shared + cut(d_inner, 32, local)
                d_average = d_average - cut(d_joined, 32, local)
        shared_low = d_shared.astype(BF16)
        d_variance = dot(u1b, shared_low)
        gc1[:, lanes] += d_shared
        gc2[:, lanes] += sum_c2
        d_square = d_variance * inv_seen[:, lanes]
        d_sum = (d_average - 2.0 * average[:, lanes] * d_variance) * inv_seen[:, lanes]
        sum_b2 = jnp.zeros((32, m), F32)
        for group, count in enumerate(counts):
            wide, thin = 64 * count, 32 * count
            d_feature = []
            for local in range(count):
                at = slice(32 * local, 32 * (local + 1))
                vis = strip_of(group, local, lanes)[1]
                feature = ff[group, at, lanes]
                d_one = ie[group, at, lanes] + vis * (d_sum + 2.0 * feature * d_square)
                kept = ee[group, 16 * local : 16 * (local + 1), lanes]
                d_one = jnp.concatenate([d_one[:16] + kept, d_one[16:]], axis=0)
                d_one = d_one * fe[group, at, lanes]
                sum_b2 = sum_b2 + d_one
                d_feature.append(d_one)
            piece = stack(d_feature).astype(BF16)
            df[group, 0:thin, lanes] = piece
            d_hidden = dot(w2_s[0:wide, 0:thin], piece) * he[group, 0:wide, lanes]
            dh[group, 0:wide, lanes] = d_hidden.astype(BF16)
        gb2[:, lanes] += sum_b2
        return shared_low

    shared_low = join([backward_tile(lanes) for lanes in lane_tiles])
    g32[97:129, :] += widen(dot(variance_low, shared_low, NT))
    for group, count in enumerate(counts):
        wide, thin, low = 64 * count, 32 * count, 16 * count
        gu2[0:thin, 0:low] += dot(ib[group, 0:thin], dl[group, 0:low], NT)
        gu1[0:thin, 0:thin] += dot(jb[group, 0:thin], di[group, 0:thin], NT)
        gw2[0:wide, 0:thin] += dot(hb[group, 0:wide], df[group, 0:thin], NT)
        gw1[:, 0:wide] += dot(xs[group], dh[group, 0:wide], NT)

    @pl.when(step == pl.num_programs(0) - 1)
    def _():
        ones = jnp.ones((8, n), BF16)
        row_of = lambda ref: widen(dot_right(ones, ref[...], NT, 3)[0:1])
        g32[0:64, :] = blocks_sum(gw2, 64, 32, views)
        g32[65:97, :] = blocks_sum(gu1, 32, 32, views)
        g16[4:36, :] = blocks_sum(gu2, 32, 16, views)
        g32[64:65, :] = row_of(gb2)
        g32[129:130, :] = row_of(gc1)
        g16[36:37, :] = row_of(gc2)
        g16[309:310, :] = row_of(gd1)
        g16[310:311, :] = row_of(gs2)
        g16[311:312, :] = jnp.where(iota((1, 128), 1) == 0, row_of(gdd), 0.0)
        total = gw1[0:36, 0:128]
        total = total + roll(gw1[STRIP : STRIP + 36, 0:128], 64)
        total = total + gw1[2 * STRIP : 2 * STRIP + 36, 128:256]
        g64[0:36, :] = jnp.where(iota((36, 128), 1) < 64, total, 0.0)
        out_ref[...] = jnp.zeros_like(out_ref)
        out_ref[0:18, :] = sum(roll(g64[pl.ds(b, 18, stride=2), :], 64 * b) for b in range(2))
        out_ref[18:51, :] += sum(roll(g32[pl.ds(b, 33, stride=4), :], 32 * b) for b in range(4))
        out_ref[50:89, :] += sum(roll(g16[pl.ds(b, 39, stride=8), :], 16 * b) for b in range(8))
        sums_ref[...] = jnp.where(
            iota(sums_ref.shape, 1) == 0, loss_s[0:1, 0:1], loss_s[0:1, 1:2]
        )


def widen(value):
    rows, width = value.shape
    return jnp.concatenate([value, jnp.zeros((rows, 128 - width), F32)], axis=1)


def run_main(me, blocks, pieces, shard, deltas, targets, ray_weight):
    rows, points = blocks[0].shape[1:]
    views = rows // STRIP
    n = CHUNK
    steps = points // n
    shards = pieces.shape[0]
    sums = (shards, -(-(shard + 2) // 128) * 128)
    whole = deltas.shape[0] // 2
    pairs = deltas.reshape(whole, 1, n)
    target_pairs = jnp.pad(
        targets.reshape(whole, 2, 3).transpose(0, 2, 1), ((0, 0), (0, 5), (0, 126))
    )
    weight_pairs = jnp.pad(ray_weight.reshape(whole, 1, 2), ((0, 0), (0, 7), (0, 126)))
    vm = pltpu.VMEM
    own = lambda t, me: (me[0] * steps + t, 0, 0)
    block = pl.BlockSpec((1, rows, n), lambda t, me: (0, 0, t))
    piece = pl.BlockSpec(pieces.shape, lambda t, me: (0, 0, 0))
    return pl.pallas_call(
        lambda *refs: main_kernel(views, shard, *refs),
        out_shape=[
            jax.ShapeDtypeStruct((96, 128), F32),
            jax.ShapeDtypeStruct(sums, F32),
        ],
        grid_spec=pltpu.PrefetchScalarGridSpec(
            num_scalar_prefetch=1,
            grid=(steps,),
            in_specs=[piece]
            + [block] * 4
            + [
                pl.BlockSpec((1, 1, n), own),
                pl.BlockSpec((1, 8, 128), own),
                pl.BlockSpec((1, 8, 128), own),
            ],
            out_specs=[
                pl.BlockSpec((96, 128), lambda t, me: (0, 0)),
                pl.BlockSpec(sums, lambda t, me: (0, 0)),
            ],
            scratch_shapes=[
                vm((120, 128), F32),
                vm((40, 128), F32),
                vm((144, 128), F32),
                vm((320, 128), F32),
                vm((4, rows, n), BF16),
                vm((4, 64 * views, n), BF16),
                vm((4, 64 * views, n), F32),
                vm((4, 32 * views, n), F32),
                vm((4, 32 * views, n), F32),
                vm((4, 32 * views, n), BF16),
                vm((4, 32 * views, n), BF16),
                vm((4, 32 * views, n), F32),
                vm((4, 16 * views, n), F32),
                vm((4, 16 * views, n), BF16),
                vm((4, 32 * views, n), BF16),
                vm((4, 32 * views, n), BF16),
                vm((4, 64 * views, n), BF16),
                vm((64 * views, 128), BF16),
                vm((32 * views, 256), BF16),
                vm((64 * views, 128), BF16),
                vm((32 * views, 128), BF16),
                vm((32 * views, 128), BF16),
                vm((16 * views, 128), BF16),
                vm((32 * views, 128), BF16),
                vm((n, n), BF16),
                vm((40, 128), F32),
                vm((136, 128), F32),
                vm((312, 128), F32),
                vm((rows, 256), F32),
                vm((64 * views, 128), F32),
                vm((32 * views, 128), F32),
                vm((32 * views, 128), F32),
                vm((32, n), F32),
                vm((32, n), F32),
                vm((16, n), F32),
                vm((16, n), F32),
                vm((16, n), F32),
                vm((8, n), F32),
                vm((8, 128), F32),
            ],
        ),
        compiler_params=pltpu.CompilerParams(vmem_limit_bytes=48 * 1024 * 1024),
    )(me, pieces, *blocks, pairs, target_pairs, weight_pairs)


def adamw(master, first_moment, second_moment, gradient, step_count):
    step_float = step_count[0].astype(F32)
    first_new = MOMENT_DECAY * first_moment + (1.0 - MOMENT_DECAY) * gradient
    second_new = SQUARE_DECAY * second_moment + (1.0 - SQUARE_DECAY) * gradient * gradient
    first_fix = 1.0 - jnp.power(MOMENT_DECAY, step_float)
    second_fix = 1.0 - jnp.power(SQUARE_DECAY, step_float)
    update = first_new / first_fix / (jnp.sqrt(second_new / second_fix) + EPSILON)
    master_new = master - LEARNING_RATE * (update + WEIGHT_DECAY * master)
    return (master_new, first_new, second_new)


def body(
    master,
    first_moment,
    second_moment,
    step_count,
    feature_maps,
    pixel_index,
    visible,
    deltas,
    targets,
    scene_id,
    scene_weight,
):
    group = lax.axis_size("views")
    shards = lax.axis_size("rays")
    assert feature_maps.shape[2] <= SEEN_BIT
    shard = master.shape[0]
    spots = [lax.axis_index("views"), lax.axis_index("rays")]
    me = jnp.stack(spots).astype(jnp.int32)
    swap = lambda size, k: [(i, i ^ k) for i in range(size)]
    rows = -(-shard // 2048) * 16
    piece = jnp.pad(master.astype(BF16), (0, rows * 128 - shard)).reshape(rows, 128)
    packed = pixel_index.T + (visible.T << SEEN_SHIFT)
    held = piece[None]
    links = shards.bit_length() - 1
    for link in range(links):
        held = jnp.concatenate([held, lax.ppermute(held, "rays", swap(shards, 1 << link))])
    far = gather_rows(packed, feature_maps, me, group, (3, 2))
    three = lax.ppermute(far[0], "views", swap(group, 3))
    two = lax.ppermute(far[1], "views", swap(group, 2))
    near = gather_rows(packed, feature_maps, me, group, (1,))
    one = lax.ppermute(near[0], "views", swap(group, 1))
    mine = gather_rows(packed, feature_maps, me, group, (0,))
    hits = (scene_id[:, None] == jnp.arange(scene_weight.shape[0])[None, :]).astype(F32)
    ray_weight = jnp.sum(hits * scene_weight.astype(F32)[None, :], axis=1)
    result, sums = run_main(me, [mine[0], one, two, three], held, shard, deltas, targets, ray_weight)
    summed = result[:89].reshape(-1)
    size = shards * shard
    if summed.shape[0] < size:
        summed = jnp.pad(summed, (0, size - summed.shape[0]))
    loss_at, far_at = shard, shard + 1
    send = jnp.concatenate([summed[:size].reshape(shards, shard), sums], axis=1)
    got = lax.all_to_all(send, "rays", 0, 0, tiled=True)
    partial = jnp.sum(got, axis=0)
    whole = partial
    for k in range(1, group):
        whole = whole + lax.ppermute(partial, "views", [(i, i ^ k) for i in range(group)])
    scaled = whole[: shard + 1] / whole[far_at : far_at + shard + 1]
    loss = scaled[loss_at]
    gradient = scaled[:shard]
    return (loss, *adamw(master, first_moment, second_moment, gradient, step_count))


def solution(mesh):
    placed = (
        P("rays"),
        P("rays"),
        P("rays"),
        P(),
        P("views", None, None),
        P("rays", "views"),
        P("rays", "views"),
        P("rays", None),
        P("rays", None),
        P("rays"),
        P(),
    )
    return jax.shard_map(
        body,
        mesh=mesh,
        in_specs=placed,
        out_specs=(P(), P("rays"), P("rays"), P("rays")),
        check_vma=False,
    )
```

profile of v0, /device:TPU:0, one launch (start us, length us, event | category | flops | bytes accessed | tf_op | source)
XLA Modules:
  0.0 60.0 jit_solution(8577456233588964726)
XLA Ops:
  0.6 0.7 %convert_element_type.17 = bf16[1423]{0:T(1024)(128)(2,1)S(1)} convert(f32[1423]{0:T(1024)} %param.11) | non-fusion elementwise | flops 1423 | bytes 8538 | tf_op jit(solution)/shard_map/convert_element_type | solution.py:726
  1.3 3.0 %collective-permute-start = (bf16[1,16,128]{2,1,0:T(8,128)(2,1)S(1)}, bf16[1,16,128]{2,1,0:T(8,128)(2,1)S(1)}, u32[]{:S(2)}, u32[]{:S(2)}) collective-permute-start(bf16[1,16,128]{2,1,0:T(8,128)(2,1)S(1)} %pad_bitcast_fusion), channel_id=1, source_target_pairs={{0,4},{4,0},{8,12},{12,8},{16,20},{20,16},{24,28},{28,24},{1,5},{5... | collective-permute-start | bytes 12296 | tf_op jit(solution)/shard_map/ppermute | solution.py:731
  4.3 0.1 pad_add_fusion.refs_0_
  4.4 0.8 %add_bitcast_fusion.refs_1_.refs_2_ = s32[3,3072]{1,0:T(4,128)S(1)} fusion(s32[3072,3]{0,1:T(4,128)} %param.16, s32[3072,3]{0,1:T(4,128)} %param.17), kind=kLoop, calls=%fused_computation.2 | loop fusion | flops 18432 | bytes 110592 | tf_op jit(solution)/shard_map/add | solution.py:727
  5.2 0.0 copy-start
  5.2 1.8 %copy-done = bf16[3,35,12032]{2,1,0:T(8,128)(2,1)S(1)} copy-done((bf16[3,35,12032]{2,1,0:T(8,128)(2,1)S(1)}, bf16[3,35,12032]{2,1,0:T(8,128)(2,1)}, u32[]{:S(2)}) %copy-start) | copy-done | bytes 2526744
  7.0 4.8 %shard_map.140 = (bf16[1,120,768]{2,1,0:T(8,128)(2,1)S(1)}, bf16[1,120,768]{2,1,0:T(8,128)(2,1)S(1)}) custom-call(s32[2]{0:T(128)S(1)} %pad_add_fusion.refs_0_, s32[3,3072]{1,0:T(4,128)S(1)} %add_bitcast_fusion.refs_1_.refs_2_, s32[3,3072]{1,0:T(4,128)S(1)} %add_bitcast_fusion.refs_1_.refs_2_, bf16[3,35,12032]{2,1,0:T(8,128)(2,1)S(1)} %copy-done), custom_call_target="tpu_custom_call" | custom-call | flops 4001366016 | bytes 2526720 | tf_op jit(solution)/shard_map/pallas_call | solution.py:139
  11.8 1.6 %collective-permute-start.4 = (bf16[1,120,768]{2,1,0:T(8,128)(2,1)S(1)}, bf16[1,120,768]{2,1,0:T(8,128)(2,1)S(1)}, u32[]{:S(2)}, u32[]{:S(2)}) collective-permute-start(bf16[1,120,768]{2,1,0:T(8,128)(2,1)S(1)} %get-tuple-element.8), channel_id=1, source_target_pairs={{0,2},{1,3},{2,0},{3,1},{4,6},{5,7},{6,4},{7,5},{8,10},{9,11},{10,... | collective-permute-start | bytes 552968 | tf_op jit(solution)/shard_map/ppermute | solution.py:734
  13.4 0.0 collective-permute-start.5
  13.4 2.8 %shard_map.139 = bf16[1,120,768]{2,1,0:T(8,128)(2,1)S(1)} custom-call(s32[2]{0:T(128)S(1)} %pad_add_fusion.refs_0_, s32[3,3072]{1,0:T(4,128)S(1)} %add_bitcast_fusion.refs_1_.refs_2_, bf16[3,35,12032]{2,1,0:T(8,128)(2,1)S(1)} %copy-done), custom_call_target="tpu_custom_call" | custom-call | flops 2000683008 | bytes 2526720 | tf_op jit(solution)/shard_map/pallas_call | solution.py:139
  16.2 0.7 %collective-permute-start.3 = (bf16[1,120,768]{2,1,0:T(8,128)(2,1)S(1)}, bf16[1,120,768]{2,1,0:T(8,128)(2,1)S(1)}, u32[]{:S(2)}, u32[]{:S(2)}) collective-permute-start(bf16[1,120,768]{2,1,0:T(8,128)(2,1)S(1)} %shard_map.139), channel_id=1, source_target_pairs={{0,1},{1,0},{2,3},{3,2},{4,5},{5,4},{6,7},{7,6},{8,9},{9,8},{10,11... | collective-permute-start | bytes 552968 | tf_op jit(solution)/shard_map/ppermute | solution.py:736
  16.9 0.0 collective-permute-done
  16.9 0.0 copy-start.7
  16.9 0.0 copy-start.5
  16.9 0.0 copy-start.2
  17.0 0.0 copy-start.1
  17.0 0.0 copy-start.3
  17.0 0.0 copy-start.4
  17.0 1.6 %collective-permute-start.1 = (bf16[2,16,128]{2,1,0:T(8,128)(2,1)S(1)}, bf16[2,16,128]{2,1,0:T(8,128)(2,1)S(1)}, u32[]{:S(2)}, u32[]{:S(2)}) collective-permute-start(bf16[2,16,128]{2,1,0:T(8,128)(2,1)S(1)} %pad_maximum_fusion.2), channel_id=1, source_target_pairs={{0,8},{4,12},{8,0},{12,4},{16,24},{20,28},{24,16},{28,20},{1,9},{5... | collective-permute-start | bytes 24584 | tf_op jit(solution)/shard_map/ppermute | solution.py:731
  18.6 2.8 %shard_map.138.refs_2_ = bf16[1,120,768]{2,1,0:T(8,128)(2,1)S(1)} custom-call(s32[2]{0:T(128)S(1)} %pad_add_fusion.refs_0_, s32[3,3072]{1,0:T(4,128)S(1)} %add_bitcast_fusion.refs_1_.refs_2_, bf16[3,35,12032]{2,1,0:T(8,128)(2,1)S(1)} %copy-done), custom_call_target="tpu_custom_call" | custom-call | flops 2000683008 | bytes 2526720 | tf_op jit(solution)/shard_map/pallas_call | solution.py:139
  21.4 0.0 copy-done.6
  21.5 0.0 collective-permute-done.1
  21.5 2.7 %collective-permute-start.2 = (bf16[4,16,128]{2,1,0:T(8,128)(2,1)S(1)}, bf16[4,16,128]{2,1,0:T(8,128)(2,1)S(1)}, u32[]{:S(2)}, u32[]{:S(2)}) collective-permute-start(bf16[4,16,128]{2,1,0:T(8,128)(2,1)S(1)} %pad_maximum_fusion.1), channel_id=1, source_target_pairs={{0,16},{4,20},{8,24},{12,28},{16,0},{20,4},{24,8},{28,12},{1,17},{... | collective-permute-start | bytes 49160 | tf_op jit(solution)/shard_map/ppermute | solution.py:731
  24.1 0.0 copy-done.7
  24.1 0.1 select_reduce_fusion
  24.2 0.1 reshape.33
  24.3 0.1 reshape.34
  24.4 0.1 reshape.32.refs_6_
  24.5 1.7 %collective-permute-done.2 = bf16[4,16,128]{2,1,0:T(8,128)(2,1)S(1)} collective-permute-done((bf16[4,16,128]{2,1,0:T(8,128)(2,1)S(1)}, bf16[4,16,128]{2,1,0:T(8,128)(2,1)S(1)}, u32[]{:S(2)}, u32[]{:S(2)}) %collective-permute-start.2) | collective-permute-done | bytes 16416 | tf_op jit(solution)/shard_map/ppermute | solution.py:731
  26.2 0.0 collective-permute-done.4.refs_4_
  26.2 0.0 collective-permute-done.5.refs_5_
  26.2 0.0 collective-permute-done.3.refs_3_
  26.2 16.3 %shard_map.141 = (f32[96,128]{1,0:T(8,128)S(1)}, f32[8,1536]{1,0:T(8,128)S(1)}) custom-call(s32[2]{0:T(128)S(1)} %pad_add_fusion.refs_0_, bf16[8,16,128]{2,1,0:T(8,128)(2,1)S(1)} %pad_maximum_fusion.refs_1_, bf16[1,120,768]{2,1,0:T(8,128)(2,1)S(1)} %shard_map.138.refs_2_, bf16[1,120,768]{2,1,0:T(8,128)(2,1)S(1)} %collective-permute-done.3.refs_3_, ...), custom_call_target="tpu_custom_call" | custom-call | tf_op jit(solution)/shard_map/pallas_call | solution.py:628
  42.6 0.1 reshape.36
  42.7 0.1 maximum_bitcast_fusion
  42.7 0.1 copy.24
  42.9 11.0 %all_to_all.9 = f32[8,1,2959]{2,1,0:T(1,128)S(1)} all-to-all(f32[8,1,2959]{2,1,0:T(1,128)S(1)} %copy.24), channel_id=1, replica_groups=mesh['rays'=8,'views'=4] {'rays'}, dimensions={0} | all-to-all | bytes 189376 | tf_op jit(solution)/shard_map/all_to_all | solution.py:747
  53.8 0.1 reduce_sum.19
  53.9 0.1 collective-permute-start.6
  54.0 1.6 %collective-permute-start.7 = (f32[2959]{0:T(1024)S(1)}, f32[2959]{0:T(1024)S(1)}, u32[]{:S(2)}, u32[]{:S(2)}) collective-permute-start(f32[2959]{0:T(1024)S(1)} %reduce_sum.19), channel_id=1, source_target_pairs={{0,2},{1,3},{2,0},{3,1},{4,6},{5,7},{6,4},{7,5},{8,10},{9,11},{10,... | collective-permute-start | bytes 35516 | tf_op jit(solution)/shard_map/ppermute | solution.py:751
  55.6 0.3 collective-permute-start.8
  56.5 0.0 collective-permute-done.6
  56.6 1.2 %collective-permute-done.7 = f32[2959]{0:T(1024)S(1)} collective-permute-done((f32[2959]{0:T(1024)S(1)}, f32[2959]{0:T(1024)S(1)}, u32[]{:S(2)}, u32[]{:S(2)}) %collective-permute-start.7) | collective-permute-done | bytes 11868 | tf_op jit(solution)/shard_map/ppermute | solution.py:751
  57.8 0.9 %collective-permute-done.8 = f32[2959]{0:T(1024)S(1)} collective-permute-done((f32[2959]{0:T(1024)S(1)}, f32[2959]{0:T(1024)S(1)}, u32[]{:S(2)}, u32[]{:S(2)}) %collective-permute-start.8) | collective-permute-done | bytes 11868 | tf_op jit(solution)/shard_map/ppermute | solution.py:751
  58.7 0.1 slice_divide_fusion
  58.8 0.6 slice.27
  59.4 0.0 copy-done.1
  59.4 0.6 %multiply_subtract_fusion = (f32[1423]{0:T(1024)}, f32[1423]{0:T(1024)}, f32[1423]{0:T(1024)}) fusion(f32[1423]{0:T(1024)S(1)} %copy-done.1, f32[]{:T(128)} %bitcast.9, f32[1424]{0:T(1024)S(1)} %slice_divide_fusion, f32[1423]{0:T(1024)S(1)} %copy-done.3, f32[1423]{0:T(1024)S(1)} %copy-done.4), kind=kLoop, calls=%fused_computation.12 | loop fusion | flops 19922 | bytes 39848 | tf_op jit(solution)/shard_map/sub | solution.py:701
  (15 shorter events, 0.1 us)
Async XLA Ops:
  1.3 15.6 %collective-permute-start = (bf16[1,16,128]{2,1,0:T(8,128)(2,1)S(1)}, bf16[1,16,128]{2,1,0:T(8,128)(2,1)S(1)}, u32[]{:S(2)}, u32[]{:S(2)}) collective-permute-start(bf16[1,16,128]{2,1,0:T(8,128)(2,1)S(1)} %pad_bitcast_fusion), channel_id=1, source_target_pairs={{0,4},{4,0},{8,12},{12,8},{16,20},{20,16},{24,28},{28,24},{1,5},{5... | collective-permute-start | bytes 12296 | tf_op jit(solution)/shard_map/ppermute | solution.py:731
  5.2 1.8 %copy-start = (bf16[3,35,12032]{2,1,0:T(8,128)(2,1)S(1)}, bf16[3,35,12032]{2,1,0:T(8,128)(2,1)}, u32[]{:S(2)}) copy-start(bf16[3,35,12032]{2,1,0:T(8,128)(2,1)} %refs_3_.1) | copy-start | bytes 7580164
  11.8 14.3 %collective-permute-start.4 = (bf16[1,120,768]{2,1,0:T(8,128)(2,1)S(1)}, bf16[1,120,768]{2,1,0:T(8,128)(2,1)S(1)}, u32[]{:S(2)}, u32[]{:S(2)}) collective-permute-start(bf16[1,120,768]{2,1,0:T(8,128)(2,1)S(1)} %get-tuple-element.8), channel_id=1, source_target_pairs={{0,2},{1,3},{2,0},{3,1},{4,6},{5,7},{6,4},{7,5},{8,10},{9,11},{10,... | collective-permute-start | bytes 552968 | tf_op jit(solution)/shard_map/ppermute | solution.py:734
  13.4 12.8 %collective-permute-start.5 = (bf16[1,120,768]{2,1,0:T(8,128)(2,1)S(1)}, bf16[1,120,768]{2,1,0:T(8,128)(2,1)S(1)}, u32[]{:S(2)}, u32[]{:S(2)}) collective-permute-start(bf16[1,120,768]{2,1,0:T(8,128)(2,1)S(1)} %get-tuple-element.9), channel_id=1, source_target_pairs={{0,3},{1,2},{2,1},{3,0},{4,7},{5,6},{6,5},{7,4},{8,11},{9,10},{10,... | collective-permute-start | bytes 552968 | tf_op jit(solution)/shard_map/ppermute | solution.py:733
  16.2 10.0 %collective-permute-start.3 = (bf16[1,120,768]{2,1,0:T(8,128)(2,1)S(1)}, bf16[1,120,768]{2,1,0:T(8,128)(2,1)S(1)}, u32[]{:S(2)}, u32[]{:S(2)}) collective-permute-start(bf16[1,120,768]{2,1,0:T(8,128)(2,1)S(1)} %shard_map.139), channel_id=1, source_target_pairs={{0,1},{1,0},{2,3},{3,2},{4,5},{5,4},{6,7},{7,6},{8,9},{9,8},{10,11... | collective-permute-start | bytes 552968 | tf_op jit(solution)/shard_map/ppermute | solution.py:736
  16.9 4.5 %copy-start.6 = (s32[8]{0:T(128)S(1)}, s32[8]{0:T(128)}, u32[]{:S(2)}) copy-start(s32[8]{0:T(128)} %param.21) | copy-start | bytes 100
  16.9 7.2 %copy-start.7 = (s32[16]{0:T(128)S(1)}, s32[16]{0:T(128)}, u32[]{:S(2)}) copy-start(s32[16]{0:T(128)} %param.20) | copy-start | bytes 196
  16.9 7.3 %copy-start.5 = (f32[16,3]{0,1:T(4,128)S(1)}, f32[16,3]{0,1:T(4,128)}, u32[]{:S(2)}) copy-start(f32[16,3]{0,1:T(4,128)} %param.19) | copy-start | bytes 580
  16.9 7.5 %copy-start.2 = (f32[16,192]{1,0:T(8,128)S(1)}, f32[16,192]{1,0:T(8,128)}, u32[]{:S(2)}) copy-start(f32[16,192]{1,0:T(8,128)} %param.18) | copy-start | bytes 36868
  17.0 42.4 %copy-start.1 = (f32[1423]{0:T(1024)S(1)}, f32[1423]{0:T(1024)}, u32[]{:S(2)}) copy-start(f32[1423]{0:T(1024)} %param.11) | copy-start | bytes 17080
  17.0 42.4 %copy-start.3 = (f32[1423]{0:T(1024)S(1)}, f32[1423]{0:T(1024)}, u32[]{:S(2)}) copy-start(f32[1423]{0:T(1024)} %param.13) | copy-start | bytes 17080
  17.0 42.4 %copy-start.4 = (f32[1423]{0:T(1024)S(1)}, f32[1423]{0:T(1024)}, u32[]{:S(2)}) copy-start(f32[1423]{0:T(1024)} %param.12) | copy-start | bytes 17080
  17.0 4.5 %collective-permute-start.1 = (bf16[2,16,128]{2,1,0:T(8,128)(2,1)S(1)}, bf16[2,16,128]{2,1,0:T(8,128)(2,1)S(1)}, u32[]{:S(2)}, u32[]{:S(2)}) collective-permute-start(bf16[2,16,128]{2,1,0:T(8,128)(2,1)S(1)} %pad_maximum_fusion.2), channel_id=1, source_target_pairs={{0,8},{4,12},{8,0},{12,4},{16,24},{20,28},{24,16},{28,20},{1,9},{5... | collective-permute-start | bytes 24584 | tf_op jit(solution)/shard_map/ppermute | solution.py:731
  21.5 4.7 %collective-permute-start.2 = (bf16[4,16,128]{2,1,0:T(8,128)(2,1)S(1)}, bf16[4,16,128]{2,1,0:T(8,128)(2,1)S(1)}, u32[]{:S(2)}, u32[]{:S(2)}) collective-permute-start(bf16[4,16,128]{2,1,0:T(8,128)(2,1)S(1)} %pad_maximum_fusion.1), channel_id=1, source_target_pairs={{0,16},{4,20},{8,24},{12,28},{16,0},{20,4},{24,8},{28,12},{1,17},{... | collective-permute-start | bytes 49160 | tf_op jit(solution)/shard_map/ppermute | solution.py:731
  53.9 2.6 %collective-permute-start.6 = (f32[2959]{0:T(1024)S(1)}, f32[2959]{0:T(1024)S(1)}, u32[]{:S(2)}, u32[]{:S(2)}) collective-permute-start(f32[2959]{0:T(1024)S(1)} %reduce_sum.19), channel_id=1, source_target_pairs={{0,1},{1,0},{2,3},{3,2},{4,5},{5,4},{6,7},{7,6},{8,9},{9,8},{10,11... | collective-permute-start | bytes 35516 | tf_op jit(solution)/shard_map/ppermute | solution.py:751
  54.0 3.8 %collective-permute-start.7 = (f32[2959]{0:T(1024)S(1)}, f32[2959]{0:T(1024)S(1)}, u32[]{:S(2)}, u32[]{:S(2)}) collective-permute-start(f32[2959]{0:T(1024)S(1)} %reduce_sum.19), channel_id=1, source_target_pairs={{0,2},{1,3},{2,0},{3,1},{4,6},{5,7},{6,4},{7,5},{8,10},{9,11},{10,... | collective-permute-start | bytes 35516 | tf_op jit(solution)/shard_map/ppermute | solution.py:751
  55.6 3.1 %collective-permute-start.8 = (f32[2959]{0:T(1024)S(1)}, f32[2959]{0:T(1024)S(1)}, u32[]{:S(2)}, u32[]{:S(2)}) collective-permute-start(f32[2959]{0:T(1024)S(1)} %reduce_sum.19), channel_id=1, source_target_pairs={{0,3},{1,2},{2,1},{3,0},{4,7},{5,6},{6,5},{7,4},{8,11},{9,10},{10,... | collective-permute-start | bytes 35516 | tf_op jit(solution)/shard_map/ppermute | solution.py:751
where the time goes:
time: 60.3 us; the launch traced here: 60 us
  Pallas kernels  26.7 us (44%)
  starting transfers between devices  11.5 us (19%)
  blocking collectives  11 us (18%)
  waiting for transfers between devices  3.84 us (6%)
  local copies, waits for them, and re-layouts  2.92 us (5%)
  other arithmetic  2.59 us (4%)
  between operations  1.53 us (3%)
    pallas_call x1, Pallas kernels, run_main(): pl.pallas_call(lambda *refs: main_kernel(views, shard, *refs), out_shape=...  16.3 us
    all_to_all x1, blocking collectives, body(): got = lax.all_to_all(send, 'rays', 0, 0, tiled=True)  11 us
    pallas_call x3, Pallas kernels, gather_rows(): pl.pallas_call(lambda *refs: gather_kernel(views, tile, count, *refs), ou...  10.4 us
    ppermute x3, starting transfers between devices, body(): lax.ppermute(held, 'rays', swap(shards, 1 << link))  7.27 us
    ppermute x3, waiting for transfers between devices, body(): lax.ppermute(partial, 'views', [(i, i ^ k) for i in range(group)])  2.15 us
    ppermute x3, starting transfers between devices, body(): lax.ppermute(partial, 'views', [(i, i ^ k) for i in range(group)])  1.92 us
    unnamed x16, local copies, waits for them, and re-layouts  1.85 us
    ppermute x3, waiting for transfers between devices, body(): lax.ppermute(held, 'rays', swap(shards, 1 << link))  1.68 us
  transfers between devices with their start and end apart: 9, of which 3 were waited for; matrix products, arithmetic and copies ran while one was open for 2% of the time, Pallas kernels for 17%

commit v1 on v0

--- a/solution.py
+++ b/solution.py
@@ -170,7 +170,8 @@
     a_ref[...] = jnp.zeros_like(a_ref)
     shards, rows, _ = shard_refs.shape
     for k in range(shards):
-        start = (place ^ k) * shard
+        owner = sum(((k >> bit) & 1) * (shards >> (bit + 1)) for bit in range(shards.bit_length()))
+        start = (place ^ owner) * shard
         shift = start & 127
         value = pltpu.roll(shard_refs[k].astype(F32), shift, 1)
         keep = iota((rows, 128), 1) >= shift
@@ -728,7 +729,7 @@
     held = piece[None]
     links = shards.bit_length() - 1
     for link in range(links):
-        held = jnp.concatenate([held, lax.ppermute(held, "rays", swap(shards, 1 << link))])
+        held = jnp.concatenate([held, lax.ppermute(held, "rays", swap(shards, shards >> (link + 1)))])
     far = gather_rows(packed, feature_maps, me, group, (3, 2))
     three = lax.ppermute(far[0], "views", swap(group, 3))
     two = lax.ppermute(far[1], "views", swap(group, 2))

time: 60.3 us -> 59.4 us (0.985)
  blocking collectives: 11 us -> 9.88 us
    all_to_all x1, blocking collectives: 11 us -> 9.88 us  [body(): got = lax.all_to_all(send, 'rays', 0, 0, tiled=True)]
  transfers between devices with their start and end apart: 9 -> 9, of which waited for: 3 -> 3; matrix products, arithmetic and copies ran while one was open for 2% -> 2% of each run, Pallas kernels for 17% -> 18%
where the time goes in v1:
time: 59.4 us; the launch traced here: 59.1 us
  Pallas kernels  26.7 us (45%)
  starting transfers between devices  11.5 us (19%)
  blocking collectives  9.88 us (17%)
  waiting for transfers between devices  4.03 us (7%)
  local copies, waits for them, and re-layouts  2.92 us (5%)
  other arithmetic  2.59 us (4%)
  between operations  1.53 us (3%)
    pallas_call x1, Pallas kernels, run_main(): pl.pallas_call(lambda *refs: main_kernel(views, shard, *refs), out_shape=...  16.3 us
    pallas_call x3, Pallas kernels, gather_rows(): pl.pallas_call(lambda *refs: gather_kernel(views, tile, count, *refs), ou...  10.4 us
    all_to_all x1, blocking collectives, body(): got = lax.all_to_all(send, 'rays', 0, 0, tiled=True)  9.88 us
    ppermute x3, starting transfers between devices, body(): lax.ppermute(held, 'rays', swap(shards, shards >> link + 1))  7.26 us
    ppermute x3, waiting for transfers between devices, body(): lax.ppermute(partial, 'views', [(i, i ^ k) for i in range(group)])  2.15 us
    ppermute x3, starting transfers between devices, body(): lax.ppermute(partial, 'views', [(i, i ^ k) for i in range(group)])  1.92 us
    ppermute x3, waiting for transfers between devices, body(): lax.ppermute(held, 'rays', swap(shards, shards >> link + 1))  1.87 us
    unnamed x16, local copies, waits for them, and re-layouts  1.85 us
  transfers between devices with their start and end apart: 9, of which 3 were waited for; matrix products, arithmetic and copies ran while one was open for 2% of the time, Pallas kernels for 18%

profile of v1, /device:TPU:0, one launch (start us, length us, event | category | flops | bytes accessed | tf_op | source)
XLA Modules:
  0.0 59.1 jit_solution(11220964233683935718)
XLA Ops:
  0.6 0.7 %convert_element_type.17 = bf16[1423]{0:T(1024)(128)(2,1)S(1)} convert(f32[1423]{0:T(1024)} %param.11) | non-fusion elementwise | flops 1423 | bytes 8538 | tf_op jit(solution)/shard_map/convert_element_type | solution.py:727
  1.3 4.1 %collective-permute-start = (bf16[1,16,128]{2,1,0:T(8,128)(2,1)S(1)}, bf16[1,16,128]{2,1,0:T(8,128)(2,1)S(1)}, u32[]{:S(2)}, u32[]{:S(2)}) collective-permute-start(bf16[1,16,128]{2,1,0:T(8,128)(2,1)S(1)} %pad_bitcast_fusion), channel_id=1, source_target_pairs={{0,16},{4,20},{8,24},{12,28},{16,0},{20,4},{24,8},{28,12},{1,17},{... | collective-permute-start | bytes 12296 | tf_op jit(solution)/shard_map/ppermute | solution.py:732
  5.4 0.1 pad_add_fusion.refs_0_
  5.5 0.8 %add_bitcast_fusion.refs_1_.refs_2_ = s32[3,3072]{1,0:T(4,128)S(1)} fusion(s32[3072,3]{0,1:T(4,128)} %param.16, s32[3072,3]{0,1:T(4,128)} %param.17), kind=kLoop, calls=%fused_computation.2 | loop fusion | flops 18432 | bytes 110592 | tf_op jit(solution)/shard_map/add | solution.py:728
  6.3 0.0 copy-start
  6.3 1.8 %copy-done = bf16[3,35,12032]{2,1,0:T(8,128)(2,1)S(1)} copy-done((bf16[3,35,12032]{2,1,0:T(8,128)(2,1)S(1)}, bf16[3,35,12032]{2,1,0:T(8,128)(2,1)}, u32[]{:S(2)}) %copy-start) | copy-done | bytes 2526744
  8.1 4.8 %shard_map.140 = (bf16[1,120,768]{2,1,0:T(8,128)(2,1)S(1)}, bf16[1,120,768]{2,1,0:T(8,128)(2,1)S(1)}) custom-call(s32[2]{0:T(128)S(1)} %pad_add_fusion.refs_0_, s32[3,3072]{1,0:T(4,128)S(1)} %add_bitcast_fusion.refs_1_.refs_2_, s32[3,3072]{1,0:T(4,128)S(1)} %add_bitcast_fusion.refs_1_.refs_2_, bf16[3,35,12032]{2,1,0:T(8,128)(2,1)S(1)} %copy-done), custom_call_target="tpu_custom_call" | custom-call | flops 4001366016 | bytes 2526720 | tf_op jit(solution)/shard_map/pallas_call | solution.py:139
  12.9 1.6 %collective-permute-start.4 = (bf16[1,120,768]{2,1,0:T(8,128)(2,1)S(1)}, bf16[1,120,768]{2,1,0:T(8,128)(2,1)S(1)}, u32[]{:S(2)}, u32[]{:S(2)}) collective-permute-start(bf16[1,120,768]{2,1,0:T(8,128)(2,1)S(1)} %get-tuple-element.8), channel_id=1, source_target_pairs={{0,2},{1,3},{2,0},{3,1},{4,6},{5,7},{6,4},{7,5},{8,10},{9,11},{10,... | collective-permute-start | bytes 552968 | tf_op jit(solution)/shard_map/ppermute | solution.py:735
  14.5 0.0 collective-permute-start.5
  14.5 2.8 %shard_map.139 = bf16[1,120,768]{2,1,0:T(8,128)(2,1)S(1)} custom-call(s32[2]{0:T(128)S(1)} %pad_add_fusion.refs_0_, s32[3,3072]{1,0:T(4,128)S(1)} %add_bitcast_fusion.refs_1_.refs_2_, bf16[3,35,12032]{2,1,0:T(8,128)(2,1)S(1)} %copy-done), custom_call_target="tpu_custom_call" | custom-call | flops 2000683008 | bytes 2526720 | tf_op jit(solution)/shard_map/pallas_call | solution.py:139
  17.3 0.7 %collective-permute-start.3 = (bf16[1,120,768]{2,1,0:T(8,128)(2,1)S(1)}, bf16[1,120,768]{2,1,0:T(8,128)(2,1)S(1)}, u32[]{:S(2)}, u32[]{:S(2)}) collective-permute-start(bf16[1,120,768]{2,1,0:T(8,128)(2,1)S(1)} %shard_map.139), channel_id=1, source_target_pairs={{0,1},{1,0},{2,3},{3,2},{4,5},{5,4},{6,7},{7,6},{8,9},{9,8},{10,11... | collective-permute-start | bytes 552968 | tf_op jit(solution)/shard_map/ppermute | solution.py:737
  18.0 0.0 collective-permute-done
  18.0 0.0 copy-start.7
  18.0 0.0 copy-start.5
  18.0 0.0 copy-start.2
  18.1 0.0 copy-start.1
  18.1 0.0 copy-start.3
  18.1 0.0 copy-start.4
  18.1 1.6 %collective-permute-start.1 = (bf16[2,16,128]{2,1,0:T(8,128)(2,1)S(1)}, bf16[2,16,128]{2,1,0:T(8,128)(2,1)S(1)}, u32[]{:S(2)}, u32[]{:S(2)}) collective-permute-start(bf16[2,16,128]{2,1,0:T(8,128)(2,1)S(1)} %pad_maximum_fusion.2), channel_id=1, source_target_pairs={{0,8},{4,12},{8,0},{12,4},{16,24},{20,28},{24,16},{28,20},{1,9},{5... | collective-permute-start | bytes 24584 | tf_op jit(solution)/shard_map/ppermute | solution.py:732
  19.7 2.8 %shard_map.138.refs_2_ = bf16[1,120,768]{2,1,0:T(8,128)(2,1)S(1)} custom-call(s32[2]{0:T(128)S(1)} %pad_add_fusion.refs_0_, s32[3,3072]{1,0:T(4,128)S(1)} %add_bitcast_fusion.refs_1_.refs_2_, bf16[3,35,12032]{2,1,0:T(8,128)(2,1)S(1)} %copy-done), custom_call_target="tpu_custom_call" | custom-call | flops 2000683008 | bytes 2526720 | tf_op jit(solution)/shard_map/pallas_call | solution.py:139
  22.5 0.0 copy-done.6
  22.5 0.0 collective-permute-done.1
  22.6 1.6 %collective-permute-start.2 = (bf16[4,16,128]{2,1,0:T(8,128)(2,1)S(1)}, bf16[4,16,128]{2,1,0:T(8,128)(2,1)S(1)}, u32[]{:S(2)}, u32[]{:S(2)}) collective-permute-start(bf16[4,16,128]{2,1,0:T(8,128)(2,1)S(1)} %pad_maximum_fusion.1), channel_id=1, source_target_pairs={{0,4},{4,0},{8,12},{12,8},{16,20},{20,16},{24,28},{28,24},{1,5},{5... | collective-permute-start | bytes 49160 | tf_op jit(solution)/shard_map/ppermute | solution.py:732
  24.1 0.0 copy-done.7
  24.1 0.1 select_reduce_fusion
  24.2 0.1 reshape.33
  24.3 0.1 reshape.34
  24.4 0.1 reshape.32.refs_6_
  24.5 1.9 %collective-permute-done.2 = bf16[4,16,128]{2,1,0:T(8,128)(2,1)S(1)} collective-permute-done((bf16[4,16,128]{2,1,0:T(8,128)(2,1)S(1)}, bf16[4,16,128]{2,1,0:T(8,128)(2,1)S(1)}, u32[]{:S(2)}, u32[]{:S(2)}) %collective-permute-start.2) | collective-permute-done | bytes 16416 | tf_op jit(solution)/shard_map/ppermute | solution.py:732
  26.4 0.0 collective-permute-done.4.refs_4_
  26.4 0.0 collective-permute-done.5.refs_5_
  26.4 0.0 collective-permute-done.3.refs_3_
  26.4 16.3 %shard_map.141 = (f32[96,128]{1,0:T(8,128)S(1)}, f32[8,1536]{1,0:T(8,128)S(1)}) custom-call(s32[2]{0:T(128)S(1)} %pad_add_fusion.refs_0_, bf16[8,16,128]{2,1,0:T(8,128)(2,1)S(1)} %pad_maximum_fusion.refs_1_, bf16[1,120,768]{2,1,0:T(8,128)(2,1)S(1)} %shard_map.138.refs_2_, bf16[1,120,768]{2,1,0:T(8,128)(2,1)S(1)} %collective-permute-done.3.refs_3_, ...), custom_call_target="tpu_custom_call" | custom-call | tf_op jit(solution)/shard_map/pallas_call | solution.py:629
  42.7 0.1 reshape.36
  42.9 0.1 maximum_bitcast_fusion
  42.9 0.1 copy.24
  43.0 9.9 %all_to_all.9 = f32[8,1,2959]{2,1,0:T(1,128)S(1)} all-to-all(f32[8,1,2959]{2,1,0:T(1,128)S(1)} %copy.24), channel_id=1, replica_groups=mesh['rays'=8,'views'=4] {'rays'}, dimensions={0} | all-to-all | bytes 189376 | tf_op jit(solution)/shard_map/all_to_all | solution.py:748
  52.9 0.1 reduce_sum.19
  53.0 0.1 collective-permute-start.6
  53.1 1.6 %collective-permute-start.7 = (f32[2959]{0:T(1024)S(1)}, f32[2959]{0:T(1024)S(1)}, u32[]{:S(2)}, u32[]{:S(2)}) collective-permute-start(f32[2959]{0:T(1024)S(1)} %reduce_sum.19), channel_id=1, source_target_pairs={{0,2},{1,3},{2,0},{3,1},{4,6},{5,7},{6,4},{7,5},{8,10},{9,11},{10,... | collective-permute-start | bytes 35516 | tf_op jit(solution)/shard_map/ppermute | solution.py:752
  54.7 0.3 collective-permute-start.8
  55.6 0.0 collective-permute-done.6
  55.6 1.2 %collective-permute-done.7 = f32[2959]{0:T(1024)S(1)} collective-permute-done((f32[2959]{0:T(1024)S(1)}, f32[2959]{0:T(1024)S(1)}, u32[]{:S(2)}, u32[]{:S(2)}) %collective-permute-start.7) | collective-permute-done | bytes 11868 | tf_op jit(solution)/shard_map/ppermute | solution.py:752
  56.9 0.9 %collective-permute-done.8 = f32[2959]{0:T(1024)S(1)} collective-permute-done((f32[2959]{0:T(1024)S(1)}, f32[2959]{0:T(1024)S(1)}, u32[]{:S(2)}, u32[]{:S(2)}) %collective-permute-start.8) | collective-permute-done | bytes 11868 | tf_op jit(solution)/shard_map/ppermute | solution.py:752
  57.8 0.1 slice_divide_fusion
  57.9 0.6 slice.27
  58.5 0.0 copy-done.1
  58.5 0.6 %multiply_subtract_fusion = (f32[1423]{0:T(1024)}, f32[1423]{0:T(1024)}, f32[1423]{0:T(1024)}) fusion(f32[1423]{0:T(1024)S(1)} %copy-done.1, f32[]{:T(128)} %bitcast.9, f32[1424]{0:T(1024)S(1)} %slice_divide_fusion, f32[1423]{0:T(1024)S(1)} %copy-done.3, f32[1423]{0:T(1024)S(1)} %copy-done.4), kind=kLoop, calls=%fused_computation.12 | loop fusion | flops 19922 | bytes 39848 | tf_op jit(solution)/shard_map/sub | solution.py:702
  (15 shorter events, 0.1 us)
Async XLA Ops:
  1.3 16.7 %collective-permute-start = (bf16[1,16,128]{2,1,0:T(8,128)(2,1)S(1)}, bf16[1,16,128]{2,1,0:T(8,128)(2,1)S(1)}, u32[]{:S(2)}, u32[]{:S(2)}) collective-permute-start(bf16[1,16,128]{2,1,0:T(8,128)(2,1)S(1)} %pad_bitcast_fusion), channel_id=1, source_target_pairs={{0,16},{4,20},{8,24},{12,28},{16,0},{20,4},{24,8},{28,12},{1,17},{... | collective-permute-start | bytes 12296 | tf_op jit(solution)/shard_map/ppermute | solution.py:732
  6.3 1.8 %copy-start = (bf16[3,35,12032]{2,1,0:T(8,128)(2,1)S(1)}, bf16[3,35,12032]{2,1,0:T(8,128)(2,1)}, u32[]{:S(2)}) copy-start(bf16[3,35,12032]{2,1,0:T(8,128)(2,1)} %refs_3_.1) | copy-start | bytes 7580164
  12.9 13.4 %collective-permute-start.4 = (bf16[1,120,768]{2,1,0:T(8,128)(2,1)S(1)}, bf16[1,120,768]{2,1,0:T(8,128)(2,1)S(1)}, u32[]{:S(2)}, u32[]{:S(2)}) collective-permute-start(bf16[1,120,768]{2,1,0:T(8,128)(2,1)S(1)} %get-tuple-element.8), channel_id=1, source_target_pairs={{0,2},{1,3},{2,0},{3,1},{4,6},{5,7},{6,4},{7,5},{8,10},{9,11},{10,... | collective-permute-start | bytes 552968 | tf_op jit(solution)/shard_map/ppermute | solution.py:735
  14.5 11.9 %collective-permute-start.5 = (bf16[1,120,768]{2,1,0:T(8,128)(2,1)S(1)}, bf16[1,120,768]{2,1,0:T(8,128)(2,1)S(1)}, u32[]{:S(2)}, u32[]{:S(2)}) collective-permute-start(bf16[1,120,768]{2,1,0:T(8,128)(2,1)S(1)} %get-tuple-element.9), channel_id=1, source_target_pairs={{0,3},{1,2},{2,1},{3,0},{4,7},{5,6},{6,5},{7,4},{8,11},{9,10},{10,... | collective-permute-start | bytes 552968 | tf_op jit(solution)/shard_map/ppermute | solution.py:734
  17.3 9.1 %collective-permute-start.3 = (bf16[1,120,768]{2,1,0:T(8,128)(2,1)S(1)}, bf16[1,120,768]{2,1,0:T(8,128)(2,1)S(1)}, u32[]{:S(2)}, u32[]{:S(2)}) collective-permute-start(bf16[1,120,768]{2,1,0:T(8,128)(2,1)S(1)} %shard_map.139), channel_id=1, source_target_pairs={{0,1},{1,0},{2,3},{3,2},{4,5},{5,4},{6,7},{7,6},{8,9},{9,8},{10,11... | collective-permute-start | bytes 552968 | tf_op jit(solution)/shard_map/ppermute | solution.py:737
  18.0 4.5 %copy-start.6 = (s32[8]{0:T(128)S(1)}, s32[8]{0:T(128)}, u32[]{:S(2)}) copy-start(s32[8]{0:T(128)} %param.21) | copy-start | bytes 100
  18.0 6.1 %copy-start.7 = (s32[16]{0:T(128)S(1)}, s32[16]{0:T(128)}, u32[]{:S(2)}) copy-start(s32[16]{0:T(128)} %param.20) | copy-start | bytes 196
  18.0 6.2 %copy-start.5 = (f32[16,3]{0,1:T(4,128)S(1)}, f32[16,3]{0,1:T(4,128)}, u32[]{:S(2)}) copy-start(f32[16,3]{0,1:T(4,128)} %param.19) | copy-start | bytes 580
  18.0 6.4 %copy-start.2 = (f32[16,192]{1,0:T(8,128)S(1)}, f32[16,192]{1,0:T(8,128)}, u32[]{:S(2)}) copy-start(f32[16,192]{1,0:T(8,128)} %param.18) | copy-start | bytes 36868
  18.1 40.4 %copy-start.1 = (f32[1423]{0:T(1024)S(1)}, f32[1423]{0:T(1024)}, u32[]{:S(2)}) copy-start(f32[1423]{0:T(1024)} %param.11) | copy-start | bytes 17080
  18.1 40.4 %copy-start.3 = (f32[1423]{0:T(1024)S(1)}, f32[1423]{0:T(1024)}, u32[]{:S(2)}) copy-start(f32[1423]{0:T(1024)} %param.13) | copy-start | bytes 17080
  18.1 40.4 %copy-start.4 = (f32[1423]{0:T(1024)S(1)}, f32[1423]{0:T(1024)}, u32[]{:S(2)}) copy-start(f32[1423]{0:T(1024)} %param.12) | copy-start | bytes 17080
  18.1 4.5 %collective-permute-start.1 = (bf16[2,16,128]{2,1,0:T(8,128)(2,1)S(1)}, bf16[2,16,128]{2,1,0:T(8,128)(2,1)S(1)}, u32[]{:S(2)}, u32[]{:S(2)}) collective-permute-start(bf16[2,16,128]{2,1,0:T(8,128)(2,1)S(1)} %pad_maximum_fusion.2), channel_id=1, source_target_pairs={{0,8},{4,12},{8,0},{12,4},{16,24},{20,28},{24,16},{28,20},{1,9},{5... | collective-permute-start | bytes 24584 | tf_op jit(solution)/shard_map/ppermute | solution.py:732
  22.6 3.8 %collective-permute-start.2 = (bf16[4,16,128]{2,1,0:T(8,128)(2,1)S(1)}, bf16[4,16,128]{2,1,0:T(8,128)(2,1)S(1)}, u32[]{:S(2)}, u32[]{:S(2)}) collective-permute-start(bf16[4,16,128]{2,1,0:T(8,128)(2,1)S(1)} %pad_maximum_fusion.1), channel_id=1, source_target_pairs={{0,4},{4,0},{8,12},{12,8},{16,20},{20,16},{24,28},{28,24},{1,5},{5... | collective-permute-start | bytes 49160 | tf_op jit(solution)/shard_map/ppermute | solution.py:732
  53.0 2.6 %collective-permute-start.6 = (f32[2959]{0:T(1024)S(1)}, f32[2959]{0:T(1024)S(1)}, u32[]{:S(2)}, u32[]{:S(2)}) collective-permute-start(f32[2959]{0:T(1024)S(1)} %reduce_sum.19), channel_id=1, source_target_pairs={{0,1},{1,0},{2,3},{3,2},{4,5},{5,4},{6,7},{7,6},{8,9},{9,8},{10,11... | collective-permute-start | bytes 35516 | tf_op jit(solution)/shard_map/ppermute | solution.py:752
  53.1 3.8 %collective-permute-start.7 = (f32[2959]{0:T(1024)S(1)}, f32[2959]{0:T(1024)S(1)}, u32[]{:S(2)}, u32[]{:S(2)}) collective-permute-start(f32[2959]{0:T(1024)S(1)} %reduce_sum.19), channel_id=1, source_target_pairs={{0,2},{1,3},{2,0},{3,1},{4,6},{5,7},{6,4},{7,5},{8,10},{9,11},{10,... | collective-permute-start | bytes 35516 | tf_op jit(solution)/shard_map/ppermute | solution.py:752
  54.7 3.1 %collective-permute-start.8 = (f32[2959]{0:T(1024)S(1)}, f32[2959]{0:T(1024)S(1)}, u32[]{:S(2)}, u32[]{:S(2)}) collective-permute-start(f32[2959]{0:T(1024)S(1)} %reduce_sum.19), channel_id=1, source_target_pairs={{0,3},{1,2},{2,1},{3,0},{4,7},{5,6},{6,5},{7,4},{8,11},{9,10},{10,... | collective-permute-start | bytes 35516 | tf_op jit(solution)/shard_map/ppermute | solution.py:752

commit v2 on v1

--- a/solution.py
+++ b/solution.py
@@ -648,9 +648,9 @@
             ],
             scratch_shapes=[
                 vm((120, 128), F32),
-                vm((40, 128), F32),
-                vm((144, 128), F32),
-                vm((320, 128), F32),
+                vm((56, 128), F32),
+                vm((168, 128), F32),
+                vm((336, 128), F32),
                 vm((4, rows, n), BF16),
                 vm((4, 64 * views, n), BF16),
                 vm((4, 64 * views, n), F32),
@@ -672,9 +672,9 @@
                 vm((16 * views, 128), BF16),
                 vm((32 * views, 128), BF16),
                 vm((n, n), BF16),
-                vm((40, 128), F32),
-                vm((136, 128), F32),
-                vm((312, 128), F32),
+                vm((56, 128), F32),
+                vm((168, 128), F32),
+                vm((336, 128), F32),
                 vm((rows, 256), F32),
                 vm((64 * views, 128), F32),
                 vm((32 * views, 128), F32),

time: 59.4 us -> 59.4 us (level)
  no operation moved by 1% of the time
where the time goes in v2:
time: 59.4 us; the launch traced here: 59.1 us
  Pallas kernels  26.7 us (45%)
  starting transfers between devices  11.5 us (19%)
  blocking collectives  9.88 us (17%)
  waiting for transfers between devices  4.03 us (7%)
  local copies, waits for them, and re-layouts  2.92 us (5%)
  other arithmetic  2.59 us (4%)
  between operations  1.53 us (3%)
    pallas_call x1, Pallas kernels, run_main(): pl.pallas_call(lambda *refs: main_kernel(views, shard, *refs), out_shape=...  16.3 us
    pallas_call x3, Pallas kernels, gather_rows(): pl.pallas_call(lambda *refs: gather_kernel(views, tile, count, *refs), ou...  10.4 us
    all_to_all x1, blocking collectives, body(): got = lax.all_to_all(send, 'rays', 0, 0, tiled=True)  9.88 us
    ppermute x3, starting transfers between devices, body(): lax.ppermute(held, 'rays', swap(shards, shards >> link + 1))  7.26 us
    ppermute x3, waiting for transfers between devices, body(): lax.ppermute(partial, 'views', [(i, i ^ k) for i in range(group)])  2.15 us
    ppermute x3, starting transfers between devices, body(): lax.ppermute(partial, 'views', [(i, i ^ k) for i in range(group)])  1.92 us
    ppermute x3, waiting for transfers between devices, body(): lax.ppermute(held, 'rays', swap(shards, shards >> link + 1))  1.87 us
    unnamed x16, local copies, waits for them, and re-layouts  1.85 us
  transfers between devices with their start and end apart: 9, of which 3 were waited for; matrix products, arithmetic and copies ran while one was open for 2% of the time, Pallas kernels for 18%

profile of v2, /device:TPU:0, one launch (start us, length us, event | category | flops | bytes accessed | tf_op | source)
XLA Modules:
  0.0 59.1 jit_solution(10822072500996157368)
XLA Ops:
  0.6 0.7 %convert_element_type.17 = bf16[1423]{0:T(1024)(128)(2,1)S(1)} convert(f32[1423]{0:T(1024)} %param.11) | non-fusion elementwise | flops 1423 | bytes 8538 | tf_op jit(solution)/shard_map/convert_element_type | solution.py:727
  1.3 4.1 %collective-permute-start = (bf16[1,16,128]{2,1,0:T(8,128)(2,1)S(1)}, bf16[1,16,128]{2,1,0:T(8,128)(2,1)S(1)}, u32[]{:S(2)}, u32[]{:S(2)}) collective-permute-start(bf16[1,16,128]{2,1,0:T(8,128)(2,1)S(1)} %pad_bitcast_fusion), channel_id=1, source_target_pairs={{0,16},{4,20},{8,24},{12,28},{16,0},{20,4},{24,8},{28,12},{1,17},{... | collective-permute-start | bytes 12296 | tf_op jit(solution)/shard_map/ppermute | solution.py:732
  5.4 0.1 pad_add_fusion.refs_0_
  5.5 0.8 %add_bitcast_fusion.refs_1_.refs_2_ = s32[3,3072]{1,0:T(4,128)S(1)} fusion(s32[3072,3]{0,1:T(4,128)} %param.16, s32[3072,3]{0,1:T(4,128)} %param.17), kind=kLoop, calls=%fused_computation.2 | loop fusion | flops 18432 | bytes 110592 | tf_op jit(solution)/shard_map/add | solution.py:728
  6.3 0.0 copy-start
  6.3 1.8 %copy-done = bf16[3,35,12032]{2,1,0:T(8,128)(2,1)S(1)} copy-done((bf16[3,35,12032]{2,1,0:T(8,128)(2,1)S(1)}, bf16[3,35,12032]{2,1,0:T(8,128)(2,1)}, u32[]{:S(2)}) %copy-start) | copy-done | bytes 2526744
  8.1 4.8 %shard_map.140 = (bf16[1,120,768]{2,1,0:T(8,128)(2,1)S(1)}, bf16[1,120,768]{2,1,0:T(8,128)(2,1)S(1)}) custom-call(s32[2]{0:T(128)S(1)} %pad_add_fusion.refs_0_, s32[3,3072]{1,0:T(4,128)S(1)} %add_bitcast_fusion.refs_1_.refs_2_, s32[3,3072]{1,0:T(4,128)S(1)} %add_bitcast_fusion.refs_1_.refs_2_, bf16[3,35,12032]{2,1,0:T(8,128)(2,1)S(1)} %copy-done), custom_call_target="tpu_custom_call" | custom-call | flops 4001366016 | bytes 2526720 | tf_op jit(solution)/shard_map/pallas_call | solution.py:139
  12.9 1.6 %collective-permute-start.4 = (bf16[1,120,768]{2,1,0:T(8,128)(2,1)S(1)}, bf16[1,120,768]{2,1,0:T(8,128)(2,1)S(1)}, u32[]{:S(2)}, u32[]{:S(2)}) collective-permute-start(bf16[1,120,768]{2,1,0:T(8,128)(2,1)S(1)} %get-tuple-element.8), channel_id=1, source_target_pairs={{0,2},{1,3},{2,0},{3,1},{4,6},{5,7},{6,4},{7,5},{8,10},{9,11},{10,... | collective-permute-start | bytes 552968 | tf_op jit(solution)/shard_map/ppermute | solution.py:735
  14.5 0.0 collective-permute-start.5
  14.5 2.8 %shard_map.139 = bf16[1,120,768]{2,1,0:T(8,128)(2,1)S(1)} custom-call(s32[2]{0:T(128)S(1)} %pad_add_fusion.refs_0_, s32[3,3072]{1,0:T(4,128)S(1)} %add_bitcast_fusion.refs_1_.refs_2_, bf16[3,35,12032]{2,1,0:T(8,128)(2,1)S(1)} %copy-done), custom_call_target="tpu_custom_call" | custom-call | flops 2000683008 | bytes 2526720 | tf_op jit(solution)/shard_map/pallas_call | solution.py:139
  17.3 0.7 %collective-permute-start.3 = (bf16[1,120,768]{2,1,0:T(8,128)(2,1)S(1)}, bf16[1,120,768]{2,1,0:T(8,128)(2,1)S(1)}, u32[]{:S(2)}, u32[]{:S(2)}) collective-permute-start(bf16[1,120,768]{2,1,0:T(8,128)(2,1)S(1)} %shard_map.139), channel_id=1, source_target_pairs={{0,1},{1,0},{2,3},{3,2},{4,5},{5,4},{6,7},{7,6},{8,9},{9,8},{10,11... | collective-permute-start | bytes 552968 | tf_op jit(solution)/shard_map/ppermute | solution.py:737
  18.0 0.0 collective-permute-done
  18.0 0.0 copy-start.7
  18.0 0.0 copy-start.5
  18.0 0.0 copy-start.2
  18.1 0.0 copy-start.1
  18.1 0.0 copy-start.3
  18.1 0.0 copy-start.4
  18.1 1.6 %collective-permute-start.1 = (bf16[2,16,128]{2,1,0:T(8,128)(2,1)S(1)}, bf16[2,16,128]{2,1,0:T(8,128)(2,1)S(1)}, u32[]{:S(2)}, u32[]{:S(2)}) collective-permute-start(bf16[2,16,128]{2,1,0:T(8,128)(2,1)S(1)} %pad_maximum_fusion.2), channel_id=1, source_target_pairs={{0,8},{4,12},{8,0},{12,4},{16,24},{20,28},{24,16},{28,20},{1,9},{5... | collective-permute-start | bytes 24584 | tf_op jit(solution)/shard_map/ppermute | solution.py:732
  19.7 2.8 %shard_map.138.refs_2_ = bf16[1,120,768]{2,1,0:T(8,128)(2,1)S(1)} custom-call(s32[2]{0:T(128)S(1)} %pad_add_fusion.refs_0_, s32[3,3072]{1,0:T(4,128)S(1)} %add_bitcast_fusion.refs_1_.refs_2_, bf16[3,35,12032]{2,1,0:T(8,128)(2,1)S(1)} %copy-done), custom_call_target="tpu_custom_call" | custom-call | flops 2000683008 | bytes 2526720 | tf_op jit(solution)/shard_map/pallas_call | solution.py:139
  22.5 0.0 copy-done.6
  22.5 0.0 collective-permute-done.1
  22.6 1.6 %collective-permute-start.2 = (bf16[4,16,128]{2,1,0:T(8,128)(2,1)S(1)}, bf16[4,16,128]{2,1,0:T(8,128)(2,1)S(1)}, u32[]{:S(2)}, u32[]{:S(2)}) collective-permute-start(bf16[4,16,128]{2,1,0:T(8,128)(2,1)S(1)} %pad_maximum_fusion.1), channel_id=1, source_target_pairs={{0,4},{4,0},{8,12},{12,8},{16,20},{20,16},{24,28},{28,24},{1,5},{5... | collective-permute-start | bytes 49160 | tf_op jit(solution)/shard_map/ppermute | solution.py:732
  24.1 0.1 select_reduce_fusion
  24.2 0.1 reshape.33
  24.3 0.1 reshape.34
  24.4 0.1 reshape.32.refs_6_
  24.5 1.9 %collective-permute-done.2 = bf16[4,16,128]{2,1,0:T(8,128)(2,1)S(1)} collective-permute-done((bf16[4,16,128]{2,1,0:T(8,128)(2,1)S(1)}, bf16[4,16,128]{2,1,0:T(8,128)(2,1)S(1)}, u32[]{:S(2)}, u32[]{:S(2)}) %collective-permute-start.2) | collective-permute-done | bytes 16416 | tf_op jit(solution)/shard_map/ppermute | solution.py:732
  26.4 0.0 collective-permute-done.4.refs_4_
  26.4 0.0 collective-permute-done.5.refs_5_
  26.4 0.0 collective-permute-done.3.refs_3_
  26.4 16.3 %shard_map.141 = (f32[96,128]{1,0:T(8,128)S(1)}, f32[8,1536]{1,0:T(8,128)S(1)}) custom-call(s32[2]{0:T(128)S(1)} %pad_add_fusion.refs_0_, bf16[8,16,128]{2,1,0:T(8,128)(2,1)S(1)} %pad_maximum_fusion.refs_1_, bf16[1,120,768]{2,1,0:T(8,128)(2,1)S(1)} %shard_map.138.refs_2_, bf16[1,120,768]{2,1,0:T(8,128)(2,1)S(1)} %collective-permute-done.3.refs_3_, ...), custom_call_target="tpu_custom_call" | custom-call | tf_op jit(solution)/shard_map/pallas_call | solution.py:629
  42.7 0.1 reshape.36
  42.8 0.1 maximum_bitcast_fusion
  42.9 0.1 copy.24
  43.0 9.9 %all_to_all.9 = f32[8,1,2959]{2,1,0:T(1,128)S(1)} all-to-all(f32[8,1,2959]{2,1,0:T(1,128)S(1)} %copy.24), channel_id=1, replica_groups=mesh['rays'=8,'views'=4] {'rays'}, dimensions={0} | all-to-all | bytes 189376 | tf_op jit(solution)/shard_map/all_to_all | solution.py:748
  52.9 0.1 reduce_sum.19
  53.0 0.1 collective-permute-start.6
  53.1 1.6 %collective-permute-start.7 = (f32[2959]{0:T(1024)S(1)}, f32[2959]{0:T(1024)S(1)}, u32[]{:S(2)}, u32[]{:S(2)}) collective-permute-start(f32[2959]{0:T(1024)S(1)} %reduce_sum.19), channel_id=1, source_target_pairs={{0,2},{1,3},{2,0},{3,1},{4,6},{5,7},{6,4},{7,5},{8,10},{9,11},{10,... | collective-permute-start | bytes 35516 | tf_op jit(solution)/shard_map/ppermute | solution.py:752
  54.7 0.3 collective-permute-start.8
  55.6 0.0 collective-permute-done.6
  55.6 1.2 %collective-permute-done.7 = f32[2959]{0:T(1024)S(1)} collective-permute-done((f32[2959]{0:T(1024)S(1)}, f32[2959]{0:T(1024)S(1)}, u32[]{:S(2)}, u32[]{:S(2)}) %collective-permute-start.7) | collective-permute-done | bytes 11868 | tf_op jit(solution)/shard_map/ppermute | solution.py:752
  56.8 0.9 %collective-permute-done.8 = f32[2959]{0:T(1024)S(1)} collective-permute-done((f32[2959]{0:T(1024)S(1)}, f32[2959]{0:T(1024)S(1)}, u32[]{:S(2)}, u32[]{:S(2)}) %collective-permute-start.8) | collective-permute-done | bytes 11868 | tf_op jit(solution)/shard_map/ppermute | solution.py:752
  57.8 0.1 slice_divide_fusion
  57.9 0.6 slice.27
  58.5 0.0 copy-done.1
  58.5 0.0 copy-done.4
  58.5 0.6 %multiply_subtract_fusion = (f32[1423]{0:T(1024)}, f32[1423]{0:T(1024)}, f32[1423]{0:T(1024)}) fusion(f32[1423]{0:T(1024)S(1)} %copy-done.1, f32[]{:T(128)} %bitcast.9, f32[1424]{0:T(1024)S(1)} %slice_divide_fusion, f32[1423]{0:T(1024)S(1)} %copy-done.3, f32[1423]{0:T(1024)S(1)} %copy-done.4), kind=kLoop, calls=%fused_computation.12 | loop fusion | flops 19922 | bytes 39848 | tf_op jit(solution)/shard_map/sub | solution.py:702
  (15 shorter events, 0.1 us)
Async XLA Ops:
  1.3 16.7 %collective-permute-start = (bf16[1,16,128]{2,1,0:T(8,128)(2,1)S(1)}, bf16[1,16,128]{2,1,0:T(8,128)(2,1)S(1)}, u32[]{:S(2)}, u32[]{:S(2)}) collective-permute-start(bf16[1,16,128]{2,1,0:T(8,128)(2,1)S(1)} %pad_bitcast_fusion), channel_id=1, source_target_pairs={{0,16},{4,20},{8,24},{12,28},{16,0},{20,4},{24,8},{28,12},{1,17},{... | collective-permute-start | bytes 12296 | tf_op jit(solution)/shard_map/ppermute | solution.py:732
  6.3 1.8 %copy-start = (bf16[3,35,12032]{2,1,0:T(8,128)(2,1)S(1)}, bf16[3,35,12032]{2,1,0:T(8,128)(2,1)}, u32[]{:S(2)}) copy-start(bf16[3,35,12032]{2,1,0:T(8,128)(2,1)} %refs_3_.1) | copy-start | bytes 7580164
  12.9 13.4 %collective-permute-start.4 = (bf16[1,120,768]{2,1,0:T(8,128)(2,1)S(1)}, bf16[1,120,768]{2,1,0:T(8,128)(2,1)S(1)}, u32[]{:S(2)}, u32[]{:S(2)}) collective-permute-start(bf16[1,120,768]{2,1,0:T(8,128)(2,1)S(1)} %get-tuple-element.8), channel_id=1, source_target_pairs={{0,2},{1,3},{2,0},{3,1},{4,6},{5,7},{6,4},{7,5},{8,10},{9,11},{10,... | collective-permute-start | bytes 552968 | tf_op jit(solution)/shard_map/ppermute | solution.py:735
  14.5 11.9 %collective-permute-start.5 = (bf16[1,120,768]{2,1,0:T(8,128)(2,1)S(1)}, bf16[1,120,768]{2,1,0:T(8,128)(2,1)S(1)}, u32[]{:S(2)}, u32[]{:S(2)}) collective-permute-start(bf16[1,120,768]{2,1,0:T(8,128)(2,1)S(1)} %get-tuple-element.9), channel_id=1, source_target_pairs={{0,3},{1,2},{2,1},{3,0},{4,7},{5,6},{6,5},{7,4},{8,11},{9,10},{10,... | collective-permute-start | bytes 552968 | tf_op jit(solution)/shard_map/ppermute | solution.py:734
  17.3 9.1 %collective-permute-start.3 = (bf16[1,120,768]{2,1,0:T(8,128)(2,1)S(1)}, bf16[1,120,768]{2,1,0:T(8,128)(2,1)S(1)}, u32[]{:S(2)}, u32[]{:S(2)}) collective-permute-start(bf16[1,120,768]{2,1,0:T(8,128)(2,1)S(1)} %shard_map.139), channel_id=1, source_target_pairs={{0,1},{1,0},{2,3},{3,2},{4,5},{5,4},{6,7},{7,6},{8,9},{9,8},{10,11... | collective-permute-start | bytes 552968 | tf_op jit(solution)/shard_map/ppermute | solution.py:737
  18.0 4.5 %copy-start.6 = (s32[8]{0:T(128)S(1)}, s32[8]{0:T(128)}, u32[]{:S(2)}) copy-start(s32[8]{0:T(128)} %param.21) | copy-start | bytes 100
  18.0 6.1 %copy-start.7 = (s32[16]{0:T(128)S(1)}, s32[16]{0:T(128)}, u32[]{:S(2)}) copy-start(s32[16]{0:T(128)} %param.20) | copy-start | bytes 196
  18.0 6.2 %copy-start.5 = (f32[16,3]{0,1:T(4,128)S(1)}, f32[16,3]{0,1:T(4,128)}, u32[]{:S(2)}) copy-start(f32[16,3]{0,1:T(4,128)} %param.19) | copy-start | bytes 580
  18.0 6.4 %copy-start.2 = (f32[16,192]{1,0:T(8,128)S(1)}, f32[16,192]{1,0:T(8,128)}, u32[]{:S(2)}) copy-start(f32[16,192]{1,0:T(8,128)} %param.18) | copy-start | bytes 36868
  18.1 40.4 %copy-start.1 = (f32[1423]{0:T(1024)S(1)}, f32[1423]{0:T(1024)}, u32[]{:S(2)}) copy-start(f32[1423]{0:T(1024)} %param.11) | copy-start | bytes 17080
  18.1 40.4 %copy-start.3 = (f32[1423]{0:T(1024)S(1)}, f32[1423]{0:T(1024)}, u32[]{:S(2)}) copy-start(f32[1423]{0:T(1024)} %param.13) | copy-start | bytes 17080
  18.1 40.4 %copy-start.4 = (f32[1423]{0:T(1024)S(1)}, f32[1423]{0:T(1024)}, u32[]{:S(2)}) copy-start(f32[1423]{0:T(1024)} %param.12) | copy-start | bytes 17080
  18.1 4.5 %collective-permute-start.1 = (bf16[2,16,128]{2,1,0:T(8,128)(2,1)S(1)}, bf16[2,16,128]{2,1,0:T(8,128)(2,1)S(1)}, u32[]{:S(2)}, u32[]{:S(2)}) collective-permute-start(bf16[2,16,128]{2,1,0:T(8,128)(2,1)S(1)} %pad_maximum_fusion.2), channel_id=1, source_target_pairs={{0,8},{4,12},{8,0},{12,4},{16,24},{20,28},{24,16},{28,20},{1,9},{5... | collective-permute-start | bytes 24584 | tf_op jit(solution)/shard_map/ppermute | solution.py:732
  22.6 3.8 %collective-permute-start.2 = (bf16[4,16,128]{2,1,0:T(8,128)(2,1)S(1)}, bf16[4,16,128]{2,1,0:T(8,128)(2,1)S(1)}, u32[]{:S(2)}, u32[]{:S(2)}) collective-permute-start(bf16[4,16,128]{2,1,0:T(8,128)(2,1)S(1)} %pad_maximum_fusion.1), channel_id=1, source_target_pairs={{0,4},{4,0},{8,12},{12,8},{16,20},{20,16},{24,28},{28,24},{1,5},{5... | collective-permute-start | bytes 49160 | tf_op jit(solution)/shard_map/ppermute | solution.py:732
  53.0 2.6 %collective-permute-start.6 = (f32[2959]{0:T(1024)S(1)}, f32[2959]{0:T(1024)S(1)}, u32[]{:S(2)}, u32[]{:S(2)}) collective-permute-start(f32[2959]{0:T(1024)S(1)} %reduce_sum.19), channel_id=1, source_target_pairs={{0,1},{1,0},{2,3},{3,2},{4,5},{5,4},{6,7},{7,6},{8,9},{9,8},{10,11... | collective-permute-start | bytes 35516 | tf_op jit(solution)/shard_map/ppermute | solution.py:752
  53.1 3.8 %collective-permute-start.7 = (f32[2959]{0:T(1024)S(1)}, f32[2959]{0:T(1024)S(1)}, u32[]{:S(2)}, u32[]{:S(2)}) collective-permute-start(f32[2959]{0:T(1024)S(1)} %reduce_sum.19), channel_id=1, source_target_pairs={{0,2},{1,3},{2,0},{3,1},{4,6},{5,7},{6,4},{7,5},{8,10},{9,11},{10,... | collective-permute-start | bytes 35516 | tf_op jit(solution)/shard_map/ppermute | solution.py:752
  54.7 3.1 %collective-permute-start.8 = (f32[2959]{0:T(1024)S(1)}, f32[2959]{0:T(1024)S(1)}, u32[]{:S(2)}, u32[]{:S(2)}) collective-permute-start(f32[2959]{0:T(1024)S(1)} %reduce_sum.19), channel_id=1, source_target_pairs={{0,3},{1,2},{2,1},{3,0},{4,7},{5,6},{6,5},{7,4},{8,11},{9,10},{10,... | collective-permute-start | bytes 35516 | tf_op jit(solution)/shard_map/ppermute | solution.py:752
